TPU v7x, 512 devices: a whole 4x8x8 slice. The times are simulated.
512 devices in a mesh: dp: 64 (over x, z, core), refl: 8 (over y).
Axes of the slice: x: 4, y: 8, z: 8, core: 2. Of those that a mesh axis runs over, the one named last changes fastest.
Arguments:
- intensities: bfloat16 [2048, 16384], P('dp', 'refl'), may hold values from -12 to 12
- observed: int32 [2048, 16384], P('dp', 'refl'), may hold values 0 or 1
- qweights: bfloat16 [2048, 16384], P('dp', 'refl'), may hold values from 0.25 to 4
- ops: int32 [4, 16384], P(None, 'refl'), may hold values from 0 to 16383, as said below
- pick: int32 [64, 64], P(None, 'dp'), may hold values from 0 to 7
Outputs:
- corr: float32 [4, 2048, 256], P(None, ('dp', 'refl'))
- returned: float32 [4, 64, 64, 4, 32], P(None, 'dp', None, None, 'refl')
Inputs may be any that keep to these rules, and one draw needn't show every extreme that they name: Each row of ops is a permutation of the reflections that maps every aligned block of 2048 reflections onto itself.
All inputs are finite; a program needn't handle non-finite values. No bound on the sum of `observed` on one device may be relied on, other than what follows from the above.
Results may differ from a plain program's by a relative error of at most 0.0084.
Values may be sent and summed in bfloat16 or wider, within the bound.
A program may use at most 64 MiB of HBM per device.

v0:
```python
import jax
import jax.numpy as jnp
from jax import lax
from jax.sharding import PartitionSpec as P

SUB = 4
NOPS = 4


def gram(left, right):
    return lax.dot_general(
        left, right, (((1,), (1,)), ((), ())), preferred_element_type=jnp.float32
    )


def collect(stacked_own, blk, part_w, part_wy, part_wyy):
    first = gram(stacked_own, part_w).reshape(3, blk, -1)
    second = gram(stacked_own[: 2 * blk], part_wy).reshape(2, blk, -1)
    third = gram(stacked_own[:blk], part_wyy)[None]
    return jnp.concatenate([first, second, third], 0)


def pearson(share):
    total_w, sum_x, sum_xx = (share[:, 0], share[:, 1], share[:, 2])
    sum_y, sum_xy, sum_yy = (share[:, 3], share[:, 4], share[:, 5])
    numer = total_w * sum_xy - sum_x * sum_y
    var_x = jnp.maximum(total_w * sum_xx - sum_x * sum_x, 0.05 * total_w * sum_xx)
    var_y = jnp.maximum(total_w * sum_yy - sum_y * sum_y, 0.05 * total_w * sum_yy)
    return numer / jnp.sqrt(var_x * var_y)


def shards(intensities, observed, qweights, ops, pick):
    blk = intensities.shape[0]
    width = intensities.shape[1]
    groups = lax.axis_size("dp")
    shares = lax.axis_size("refl")
    weights = observed.astype(jnp.float32) * qweights.astype(jnp.float32)
    values = intensities.astype(jnp.float32)
    own_w = weights.astype(jnp.bfloat16)
    own_wx = (weights * values).astype(jnp.bfloat16)
    own_wxx = (weights * values * values).astype(jnp.bfloat16)
    stacked_own = jnp.concatenate([own_w, own_wx, own_wxx], 0)
    local_ops = ops - lax.axis_index("refl") * width
    request = pick[:, 0][:, None] * SUB + jnp.arange(SUB, dtype=jnp.int32)[None, :]
    send_x = intensities[request]
    send_w = own_w[request]
    got_x = lax.all_to_all(send_x, "dp", split_axis=0, concat_axis=0, tiled=True)
    got_w = lax.all_to_all(send_w, "dp", split_axis=0, concat_axis=0, tiled=True)
    count = got_x.shape[1]
    flat_x = got_x.reshape(-1, width)
    flat_w = got_w.reshape(-1, width)
    per_op = []
    for k in range(NOPS):
        perm = local_ops[k]
        moved_w = jnp.take(flat_w, perm, axis=1)
        wide_w = moved_w.astype(jnp.float32)
        wide_x = jnp.take(flat_x, perm, axis=1).astype(jnp.float32)
        moved_wy = (wide_w * wide_x).astype(jnp.bfloat16)
        moved_wyy = (wide_w * wide_x * wide_x).astype(jnp.bfloat16)
        per_op.append(collect(stacked_own, blk, moved_w, moved_wy, moved_wyy))
    stats = jnp.stack(per_op, 0)
    stats = stats.reshape(NOPS, 6, blk, groups, count)
    flat_stats = stats.reshape(NOPS, 6, blk, -1)
    rows = blk // shares
    totals = lax.psum(flat_stats, "refl")
    share = lax.dynamic_slice_in_dim(totals, lax.axis_index("refl") * rows, rows, 2)
    corr = pearson(share)
    outgoing = jnp.transpose(corr.reshape(NOPS, rows, groups, SUB), (0, 2, 3, 1))[:, :, None]
    returned = lax.all_to_all(outgoing, "dp", split_axis=1, concat_axis=2, tiled=True)
    return (corr, returned)


def solution(mesh):
    return jax.shard_map(
        shards,
        mesh=mesh,
        in_specs=(
            P("dp", "refl"),
            P("dp", "refl"),
            P("dp", "refl"),
            P(None, "refl"),
            P(None, "dp"),
        ),
        out_specs=(P(None, ("dp", "refl"), None), P(None, "dp", None, None, "refl")),
        check_vma=False,
    )
```

profile of v0, /device:TPU:1, one launch (start us, length us, event | category | flops | bytes accessed | tf_op | source)
XLA Modules:
  0.0 299.3 jit_solution(15204998179728151762)
XLA Ops:
  8.0 3.3 %gather_fusion.1 = bf16[256,2048]{1,0:T(8,128)(2,1)S(1)} fusion(bf16[32,2048]{1,0:T(8,128)(2,1)} %param.7, s32[1024]{0:T(1024)S(1)} %pad_clamp_fusion), kind=kCustom, calls=%fused_computation.9 | custom fusion | bytes 2098176 | tf_op jit(solution)/shard_map/gather | solution.py:45
  11.3 1.2 reshape.180
  12.5 15.0 %all-to-all-start.1 = ((bf16[64,4,2048]{2,1,0:T(4,128)(2,1)}), bf16[64,4,2048]{2,1,0:T(4,128)(2,1)S(1)}, u32[]{:S(2)}, u32[]{:S(2)}) async-start(bf16[64,4,2048]{2,1,0:T(4,128)(2,1)} %reshape.180), calls=%async_computation.1 | async-start | bytes 2097152 | tf_op jit(solution)/shard_map/all_to_all | solution.py:47
  27.6 1.4 gather_fusion
  29.0 1.2 reshape.172
  30.2 25.8 %all-to-all-done.1 = bf16[64,4,2048]{2,1,0:T(4,128)(2,1)S(1)} async-done(((bf16[64,4,2048]{2,1,0:T(4,128)(2,1)}), bf16[64,4,2048]{2,1,0:T(4,128)(2,1)S(1)}, u32[]{:S(2)}, u32[]{:S(2)}) %all-to-all-start.1) | async-done | bytes 1048608 | tf_op jit(solution)/shard_map/all_to_all | solution.py:47
  56.0 6.2 %all-to-all-start = ((bf16[64,4,2048]{2,1,0:T(4,128)(2,1)}), bf16[64,4,2048]{2,1,0:T(4,128)(2,1)S(1)}, u32[]{:S(2)}, u32[]{:S(2)}) async-start(bf16[64,4,2048]{2,1,0:T(4,128)(2,1)} %reshape.172), calls=%async_computation | async-start | bytes 2097152 | tf_op jit(solution)/shard_map/all_to_all | solution.py:48
  66.9 23.8 %all-to-all-done = bf16[64,4,2048]{2,1,0:T(4,128)(2,1)S(1)} async-done(((bf16[64,4,2048]{2,1,0:T(4,128)(2,1)}), bf16[64,4,2048]{2,1,0:T(4,128)(2,1)S(1)}, u32[]{:S(2)}, u32[]{:S(2)}) %all-to-all-start) | async-done | bytes 1048608 | tf_op jit(solution)/shard_map/all_to_all | solution.py:48
  91.6 9.8 %gather_fusion.7 = bf16[2048,256]{1,0:T(8,128)(2,1)} fusion(bf16[256,2048]{0,1:T(8,128)(2,1)S(1)} %copy.19, s32[2048]{0:T(1024)} %fusion.54), kind=kCustom, calls=%fused_computation.5.clone | custom fusion | bytes 2105344 | tf_op jit(solution)/shard_map/jit(_take)/gather | solution.py:57
  101.3 8.5 %gather_fusion.6 = bf16[2048,256]{1,0:T(8,128)(2,1)S(1)} fusion(bf16[256,2048]{0,1:T(8,128)(2,1)S(1)} %copy.18, s32[2048]{0:T(1024)} %fusion.54), kind=kCustom, calls=%fused_computation.4.clone | custom fusion | bytes 2105344 | tf_op jit(solution)/shard_map/jit(_take)/gather | solution.py:55
  109.8 9.7 %gather_fusion.9 = bf16[2048,256]{1,0:T(8,128)(2,1)} fusion(bf16[256,2048]{0,1:T(8,128)(2,1)S(1)} %copy.19, s32[2048]{0:T(1024)} %fusion.55), kind=kCustom, calls=%fused_computation.7.clone | custom fusion | bytes 2105344 | tf_op jit(solution)/shard_map/jit(_take)/gather | solution.py:57
  119.5 9.8 %gather_fusion.8 = bf16[2048,256]{1,0:T(8,128)(2,1)} fusion(bf16[256,2048]{0,1:T(8,128)(2,1)S(1)} %copy.18, s32[2048]{0:T(1024)} %fusion.55), kind=kCustom, calls=%fused_computation.6.clone | custom fusion | bytes 2105344 | tf_op jit(solution)/shard_map/jit(_take)/gather | solution.py:55
  129.3 2.6 convolution_bitcast_fusion.1
  132.0 1.2 fusion.12
  133.5 1.3 convolution_bitcast_fusion
  134.8 1.2 fusion.14
  136.0 1.2 fusion.30
  137.2 1.2 fusion.24
  138.3 9.0 %gather_fusion.3 = bf16[2048,256]{1,0:T(8,128)(2,1)} fusion(bf16[256,2048]{0,1:T(8,128)(2,1)S(1)} %copy.19, s32[2048]{0:T(1024)S(1)} %fusion.52), kind=kCustom, calls=%fused_computation.1.clone | custom fusion | bytes 2105344 | tf_op jit(solution)/shard_map/jit(_take)/gather | solution.py:57
  147.3 7.5 %gather_fusion.2 = bf16[2048,256]{1,0:T(8,128)(2,1)S(1)} fusion(bf16[256,2048]{0,1:T(8,128)(2,1)S(1)} %copy.18, s32[2048]{0:T(1024)S(1)} %fusion.52), kind=kCustom, calls=%fused_computation.clone | custom fusion | bytes 2105344 | tf_op jit(solution)/shard_map/jit(_take)/gather | solution.py:55
  154.9 2.6 convolution_bitcast_fusion.3
  157.5 1.3 fusion.8
  158.8 1.2 fusion.42
  159.9 7.5 %gather_fusion.5 = bf16[2048,256]{1,0:T(8,128)(2,1)S(1)} fusion(bf16[256,2048]{0,1:T(8,128)(2,1)S(1)} %copy.19, s32[2048]{0:T(1024)S(1)} %fusion.53), kind=kCustom, calls=%fused_computation.3.clone | custom fusion | bytes 2105344 | tf_op jit(solution)/shard_map/jit(_take)/gather | solution.py:57
  167.4 7.7 %gather_fusion.4 = bf16[2048,256]{1,0:T(8,128)(2,1)S(1)} fusion(bf16[256,2048]{0,1:T(8,128)(2,1)S(1)} %copy.18, s32[2048]{0:T(1024)S(1)} %fusion.53), kind=kCustom, calls=%fused_computation.2.clone | custom fusion | bytes 2105344 | tf_op jit(solution)/shard_map/jit(_take)/gather | solution.py:55
  177.6 1.0 pad_maximum_fusion
  178.6 72.0 %all-reduce.2.cloned.1.call-done = f32[4,6,32,256]{3,2,0,1:T(8,128)} async-done(((f32[4,6,32,256]{3,2,0,1:T(8,128)}), f32[4,6,32,256]{3,2,0,1:T(8,128)}) %all-reduce.2.cloned.1.call-update) | async-done | bytes 786448 | tf_op jit(solution)/shard_map/psum | solution.py:65
  250.7 1.5 fusion.50
  255.4 1.4 squeeze.43
  256.8 1.4 multiply_bitcast_fusion
  258.6 33.0 %all_to_all.22 = f32[4,64,1,4,4]{3,4,0,2,1:T(4,128)S(1)} all-to-all(f32[4,64,1,4,4]{3,4,0,2,1:T(4,128)S(1)} %copy.26), channel_id=1, replica_groups=mesh['dp'=64,'refl'=8] {'dp'}, dimensions={1} | all-to-all | bytes 32768 | tf_op jit(solution)/shard_map/all_to_all | solution.py:69
  291.5 0.9 copy.27
  (75 shorter events, 12.6 us)
Async XLA Ops:
  12.5 15.0 %copy-start = (bf16[32,2048]{1,0:T(8,128)(2,1)S(1)}, bf16[32,2048]{1,0:T(8,128)(2,1)}, u32[]{:S(2)}) copy-start(bf16[32,2048]{1,0:T(8,128)(2,1)} %param.7) | copy-start | bytes 393220
  12.5 15.0 %copy-start.5 = (s32[32,2048]{1,0:T(8,128)S(1)}, s32[32,2048]{1,0:T(8,128)}, u32[]{:S(2)}) copy-start(s32[32,2048]{1,0:T(8,128)} %param.8) | copy-start | bytes 786436
  12.5 15.0 %copy-start.6 = (bf16[32,2048]{1,0:T(8,128)(2,1)S(1)}, bf16[32,2048]{1,0:T(8,128)(2,1)}, u32[]{:S(2)}) copy-start(bf16[32,2048]{1,0:T(8,128)(2,1)} %param.9) | copy-start | bytes 393220
  12.5 43.5 %all-to-all-start.1 = ((bf16[64,4,2048]{2,1,0:T(4,128)(2,1)}), bf16[64,4,2048]{2,1,0:T(4,128)(2,1)S(1)}, u32[]{:S(2)}, u32[]{:S(2)}) async-start(bf16[64,4,2048]{2,1,0:T(4,128)(2,1)} %reshape.180), calls=%async_computation.1 | async-start | bytes 2097152 | tf_op jit(solution)/shard_map/all_to_all | solution.py:47
  29.0 1.2 copy-start.16
  56.0 34.7 %all-to-all-start = ((bf16[64,4,2048]{2,1,0:T(4,128)(2,1)}), bf16[64,4,2048]{2,1,0:T(4,128)(2,1)S(1)}, u32[]{:S(2)}, u32[]{:S(2)}) async-start(bf16[64,4,2048]{2,1,0:T(4,128)(2,1)} %reshape.172), calls=%async_computation | async-start | bytes 2097152 | tf_op jit(solution)/shard_map/all_to_all | solution.py:48
  62.2 188.4 %all-reduce.2.cloned.1.call-start = ((), (), s32[]{:S(2)}) async-start(), calls=%async_computation.3 | async-start | bytes 1572864 | tf_op jit(solution)/shard_map/psum | solution.py:65
  129.3 2.6 copy-start.2
  129.3 2.6 copy-start.20
  132.0 1.3 copy-start.1
  132.0 1.5 copy-start.3
  132.0 1.5 copy-start.19
  154.8 2.7 copy-start.4
  154.9 2.7 copy-start.18
  167.4 7.7 %copy-start.17 = (pred[2048]{0:T(1024)(128)(4,1)S(1)}, pred[2048]{0:T(1024)(128)(4,1)}, u32[]{:S(2)}) copy-start(pred[2048]{0:T(1024)(128)(4,1)} %compare_and_fusion.2) | copy-start | bytes 6148
  176.5 0.9 copy-start.7
  176.5 0.9 copy-start.8
  176.5 0.9 copy-start.10
  176.5 0.9 copy-start.11
  176.5 0.9 copy-start.13
  176.5 0.9 copy-start.14
  176.5 1.0 copy-start.9
  176.6 1.0 copy-start.12
  176.6 1.0 copy-start.15
Sparse Core Ops, SparseCore 0:
  178.8 71.8 all-reduce.1
where the time goes:
time: 301 us; the launch traced here: 299 us
  waiting for transfers between devices  122 us (41%)
  local copies, waits for them, and re-layouts  84.9 us (28%)
  blocking collectives  33 us (11%)
  starting transfers between devices  21.4 us (7%)
  matrix products  15.6 us (5%)
  between operations  14.4 us (5%)
  other arithmetic  8.37 us (3%)
    psum x1, waiting for transfers between devices, shards(): totals = lax.psum(flat_stats, 'refl')  72 us
    gather x4, local copies, waits for them, and re-layouts, shards(): wide_x = jnp.take(flat_x, perm, axis=1).astype(jnp.float32)  36 us
    gather x4, local copies, waits for them, and re-layouts, shards(): moved_w = jnp.take(flat_w, perm, axis=1)  33.5 us
    all_to_all x1, blocking collectives, shards(): lax.all_to_all(outgoing, 'dp', split_axis=1, concat_axis=2, tiled=True)  33 us
    all_to_all x1, waiting for transfers between devices, shards(): lax.all_to_all(send_x, 'dp', split_axis=0, concat_axis=0, tiled=True)  25.8 us
    all_to_all x1, waiting for transfers between devices, shards(): lax.all_to_all(send_w, 'dp', split_axis=0, concat_axis=0, tiled=True)  23.8 us
    dot_general x12, matrix products, gram(): lax.dot_general(left, right, (((1,), (1,)), ((), ())), preferred_element_...  15.6 us
    all_to_all x1, starting transfers between devices, shards(): lax.all_to_all(send_x, 'dp', split_axis=0, concat_axis=0, tiled=True)  15 us
  transfers between devices with their start and end apart: 3, of which 3 were waited for; matrix products, arithmetic and copies ran while one was open for 2% of the time, Pallas kernels for 0%

commit v1 on v0

v1 whole, which is shorter than its diff:
```python
import jax
import jax.numpy as jnp
from jax import lax
from jax.sharding import PartitionSpec as P

SUB = 4
NOPS = 4


def gram(left, right):
    return lax.dot_general(
        left, right, (((1,), (1,)), ((), ())), preferred_element_type=jnp.float32
    )


def pearson(total_w, sum_x, sum_xx, sum_y, sum_xy, sum_yy):
    numer = total_w * sum_xy - sum_x * sum_y
    var_x = jnp.maximum(total_w * sum_xx - sum_x * sum_x, 0.05 * total_w * sum_xx)
    var_y = jnp.maximum(total_w * sum_yy - sum_y * sum_y, 0.05 * total_w * sum_yy)
    return numer / jnp.sqrt(var_x * var_y)


def shards(intensities, observed, qweights, ops, pick):
    blk, width = intensities.shape
    groups = lax.axis_size("dp")
    shares = lax.axis_size("refl")
    rows = blk // shares
    own_w = (observed.astype(jnp.float32) * qweights.astype(jnp.float32)).astype(jnp.bfloat16)
    both = jnp.concatenate([intensities, own_w], 0)
    request = pick[:, 0][:, None] * SUB + jnp.arange(SUB, dtype=jnp.int32)[None, :]
    request = jnp.concatenate([request, request + blk], 1).reshape(-1)
    chosen = (request[:, None] == jnp.arange(2 * blk, dtype=jnp.int32)[None, :]).astype(jnp.bfloat16)
    send = jnp.dot(chosen, both, preferred_element_type=jnp.float32).astype(jnp.bfloat16)
    send = send.reshape(groups, 2 * SUB, width)
    got = lax.all_to_all(send, "dp", split_axis=0, concat_axis=0, tiled=True)
    local_ops = ops - lax.axis_index("refl") * width
    place = (local_ops[:, None, :] == jnp.arange(width, dtype=jnp.int32)[None, :, None]).astype(jnp.bfloat16)
    moved = jnp.einsum("ih,kgh->kig", both, place, preferred_element_type=jnp.float32)
    moved_x = moved[:, :blk]
    moved_w = moved[:, blk:]
    left_w = moved_w.astype(jnp.bfloat16).reshape(NOPS * blk, width)
    left_wx = (moved_w * moved_x).astype(jnp.bfloat16).reshape(NOPS * blk, width)
    left_wxx = (moved_w * moved_x * moved_x).astype(jnp.bfloat16).reshape(NOPS * blk, width)
    left = jnp.concatenate([left_w, left_wx, left_wxx], 0)
    got_x = got[:, :SUB].reshape(groups * SUB, width).astype(jnp.float32)
    got_w = got[:, SUB:].reshape(groups * SUB, width)
    wide_w = got_w.astype(jnp.float32)
    right_wy = (wide_w * got_x).astype(jnp.bfloat16)
    right_wyy = (wide_w * got_x * got_x).astype(jnp.bfloat16)
    n = NOPS * blk
    first = gram(left, got_w)
    second = gram(left[: 2 * n], right_wy)
    third = gram(left[:n], right_wyy)
    stats = jnp.concatenate([first, second, third], 0)
    stats = stats.reshape(6 * NOPS, shares, rows, groups * SUB)
    share = lax.psum_scatter(stats, "refl", scatter_dimension=1, tiled=False)
    share = share.reshape(6, NOPS, rows, groups * SUB)
    corr = pearson(*[share[i] for i in range(6)])
    outgoing = jnp.transpose(corr.reshape(NOPS, rows, groups, SUB), (0, 2, 3, 1))[:, :, None]
    returned = lax.all_to_all(outgoing, "dp", split_axis=1, concat_axis=2, tiled=True)
    return (corr, returned)


def solution(mesh):
    return jax.shard_map(
        shards,
        mesh=mesh,
        in_specs=(
            P("dp", "refl"),
            P("dp", "refl"),
            P("dp", "refl"),
            P(None, "refl"),
            P(None, "dp"),
        ),
        out_specs=(P(None, ("dp", "refl"), None), P(None, "dp", None, None, "refl")),
        check_vma=False,
    )
```

time: 301 us -> 178 us (0.59)
  local copies, waits for them, and re-layouts: 84.9 us -> 15.4 us
  waiting for transfers between devices: 122 us -> 85.5 us
  blocking collectives: 33 us -> 0 us
  starting transfers between devices: 21.4 us -> 30.8 us
  matrix products: 15.6 us -> 21 us
    gather x12 -> x0, local copies, waits for them, and re-layouts: 76.5 us -> none  [the longest x4 36 us: shards(): wide_x = jnp.take(flat_x, perm, axis=1).astype(jnp.float32)]
    psum x1 -> x0, waiting for transfers between devices: 72 us -> none  [shards(): totals = lax.psum(flat_stats, 'refl')]
    all_to_all x1 -> x0, blocking collectives: 33 us -> none  [shards(): lax.all_to_all(outgoing, 'dp', split_axis=1, concat_axis=2, tiled=True)]
    reduce_scatter x0 -> x1, waiting for transfers between devices: none -> 32.5 us  [shards(): share = lax.psum_scatter(stats, 'refl', scatter_dimension=1, tiled=False)]
    dot_general x0 -> x2, matrix products: none -> 16.7 us  [the longest x1 13.7 us: shards(): jnp.einsum('ih,kgh->kig', both, place, preferred_element_type=jnp.float32)]
    dot_general x12 -> x3, matrix products: 15.6 us -> 4.35 us  [gram(): lax.dot_general(left, right, (((1,), (1,)), ((), ())), preferred_element_...]
    all_to_all x2, starting transfers between devices: 21.2 us -> 30.8 us  [the longest x1 15.8 us: shards(): lax.all_to_all(outgoing, 'dp', split_axis=1, concat_axis=2, tiled=True)]
    convert_element_type x0 -> x2, local copies, waits for them, and re-layouts: none -> 4.11 us  [the longest x1 2.14 us: shards(): right_wyy = (wide_w * got_x * got_x).astype(jnp.bfloat16)]
  transfers between devices with their start and end apart: 3 -> 3, of which waited for: 3 -> 3; matrix products, arithmetic and copies ran while one was open for 2% -> 9% of each run, Pallas kernels for 0% -> 0%
where the time goes in v1:
time: 178 us; the launch traced here: 177 us
  waiting for transfers between devices  85.5 us (48%)
  starting transfers between devices  30.8 us (17%)
  matrix products  21 us (12%)
  local copies, waits for them, and re-layouts  15.4 us (9%)
  between operations  14.3 us (8%)
  other arithmetic  10.2 us (6%)
    all_to_all x1, waiting for transfers between devices, shards(): got = lax.all_to_all(send, 'dp', split_axis=0, concat_axis=0, tiled=True)  36.3 us
    reduce_scatter x1, waiting for transfers between devices, shards(): share = lax.psum_scatter(stats, 'refl', scatter_dimension=1, tiled=False)  32.5 us
    all_to_all x1, waiting for transfers between devices, shards(): lax.all_to_all(outgoing, 'dp', split_axis=1, concat_axis=2, tiled=True)  16.7 us
    all_to_all x1, starting transfers between devices, shards(): lax.all_to_all(outgoing, 'dp', split_axis=1, concat_axis=2, tiled=True)  15.8 us
    all_to_all x1, starting transfers between devices, shards(): got = lax.all_to_all(send, 'dp', split_axis=0, concat_axis=0, tiled=True)  15 us
    dot_general x1, matrix products, shards(): jnp.einsum('ih,kgh->kig', both, place, preferred_element_type=jnp.float32)  13.7 us
    dot_general x3, matrix products, gram(): lax.dot_general(left, right, (((1,), (1,)), ((), ())), preferred_element_...  4.35 us
  transfers between devices with their start and end apart: 3, of which 3 were waited for; matrix products, arithmetic and copies ran while one was open for 9% of the time, Pallas kernels for 0%

profile of v1, /device:TPU:1, one launch (start us, length us, event | category | flops | bytes accessed | tf_op | source)
XLA Modules:
  0.0 177.2 jit_solution(17554218045761646144)
XLA Ops:
  7.2 0.7 multiply_bitcast_fusion.1
  8.0 1.1 multiply_convert_fusion.3
  9.1 3.0 %fusion.2 = bf16[64,8,2048]{2,1,0:T(8,128)(2,1)} fusion(bf16[32,2048]{1,0:T(8,128)(2,1)S(1)} %multiply_convert_fusion.3, bf16[32,2048]{1,0:T(8,128)(2,1)} %param.5, s32[512]{0:T(512)S(1)} %eq.31), kind=kOutput, calls=%fused_computation.5 | convolution fusion | flops 135823360 | bytes 2361344 | tf_op jit(solution)/shard_map/dot_general | solution.py:33
  12.1 15.0 %all-to-all-start = ((bf16[64,8,2048]{2,1,0:T(8,128)(2,1)}), bf16[64,8,2048]{2,1,0:T(8,128)(2,1)S(1)}, u32[]{:S(2)}, u32[]{:S(2)}) async-start(bf16[64,8,2048]{2,1,0:T(8,128)(2,1)} %fusion.2), calls=%async_computation | async-start | bytes 4194304 | tf_op jit(solution)/shard_map/all_to_all | solution.py:35
  27.1 13.7 %fusion.3 = f32[4,64,2048]{2,1,0:T(8,128)S(1)} fusion(s32[4,2048]{1,0:T(4,128)S(1)} %broadcast_subtract_fusion, bf16[32,2048]{1,0:T(8,128)(2,1)S(1)} %multiply_convert_fusion.3, bf16[32,2048]{1,0:T(8,128)(2,1)S(1)} %copy-done.1), kind=kOutput, calls=%fused_computation.6 | convolution fusion | flops 2164785152 | bytes 2392064 | tf_op jit(solution)/shard_map/ih,kgh->kig/dot_general | solution.py:38
  40.9 1.0 multiply_convert_fusion.2
  41.9 36.3 %all-to-all-done = bf16[64,8,2048]{2,1,0:T(8,128)(2,1)S(1)} async-done(((bf16[64,8,2048]{2,1,0:T(8,128)(2,1)}), bf16[64,8,2048]{2,1,0:T(8,128)(2,1)S(1)}, u32[]{:S(2)}, u32[]{:S(2)}) %all-to-all-start) | async-done | bytes 2097184 | tf_op jit(solution)/shard_map/all_to_all | solution.py:35
  78.2 1.8 %fusion.4 = bf16[64,4,2048]{2,1,0:T(4,128)(2,1)} fusion(bf16[64,8,2048]{2,1,0:T(8,128)(2,1)S(1)} %all-to-all-done), kind=kLoop, calls=%fused_computation.7 | loop fusion | flops 2621440 | bytes 3145728 | tf_op jit(solution)/shard_map/convert_element_type | solution.py:49
  80.0 2.1 %convert_element_type.61 = bf16[256,2048]{1,0:T(8,128)(2,1)} reshape(bf16[64,4,2048]{2,1,0:T(4,128)(2,1)} %fusion.4) | data formatting | bytes 2097152 | tf_op jit(solution)/shard_map/convert_element_type | solution.py:49
  82.2 2.5 %fusion.27 = (bf16[64,4,2048]{2,1,0:T(4,128)(2,1)}, f32[64,4,2048]{2,1,0:T(4,128)}) fusion(bf16[64,8,2048]{2,1,0:T(8,128)(2,1)S(1)} %all-to-all-done), kind=kLoop, calls=%fused_computation.56 | loop fusion | flops 524288 | bytes 5242880 | tf_op jit(solution)/shard_map/slice | solution.py:46
  84.6 2.2 %reshape.60 = bf16[256,2048]{1,0:T(8,128)(2,1)} reshape(bf16[64,4,2048]{2,1,0:T(4,128)(2,1)} %get-tuple-element.10) | data formatting | bytes 2097152 | tf_op jit(solution)/shard_map/reshape | solution.py:46
  86.8 2.0 %reshape.62 = f32[256,2048]{1,0:T(8,128)S(1)} reshape(f32[64,4,2048]{2,1,0:T(4,128)} %get-tuple-element.11) | data formatting | bytes 4194304 | tf_op jit(solution)/shard_map/convert_element_type | solution.py:45
  88.8 1.7 fusion.29
  90.5 2.1 %fusion.5 = f32[384,256]{1,0:T(8,128)S(1)} fusion(bf16[256,2048]{1,0:T(8,128)(2,1)} %reshape.60, bf16[128,2048]{1,0:T(8,128)(2,1)} %bitcast.80, bf16[128,2048]{1,0:T(8,128)(2,1)S(1)} %bitcast.77, bf16[128,2048]{1,0:T(8,128)(2,1)S(1)} %bitcast.75), kind=kOutput, calls=%fused_computation.9 | convolution fusion | flops 407371776 | bytes 3014656 | tf_op jit(solution)/shard_map/dot_general | solution.py:11
  92.6 0.6 fusion.11
  93.5 1.3 copy.11
  94.8 32.5 %reduce-scatter.2.cloned.1.call-done = f32[24,1,4,256]{3,0,2,1:T(8,128)} async-done(((f32[24,8,4,256]{3,0,2,1:T(8,128)}), f32[24,1,4,256]{3,0,2,1:T(8,128)}) %reduce-scatter.2.cloned.1.call-update) | async-done | bytes 98320 | tf_op jit(solution)/shard_map/reduce_scatter | solution.py:56
  127.3 0.9 fusion.28
  128.3 0.9 fusion.21
  129.2 0.5 mul.126
  129.7 0.5 squeeze.26
  130.2 0.5 mul.128
  130.8 0.5 squeeze.28
  131.3 0.5 squeeze.29
  131.9 0.5 mul.132
  132.4 1.4 squeeze.27
  133.8 1.4 multiply_bitcast_fusion
  135.2 1.1 copy.19
  136.4 15.8 %all-to-all-start.1 = ((f32[4,64,1,4,4]{3,4,0,2,1:T(4,128)}), f32[4,64,1,4,4]{3,4,0,2,1:T(4,128)S(1)}, u32[]{:S(2)}, u32[]{:S(2)}) async-start(f32[4,64,1,4,4]{3,4,0,2,1:T(4,128)} %copy.19), calls=%async_computation.2 | async-start | bytes 1048576 | tf_op jit(solution)/shard_map/all_to_all | solution.py:60
  152.2 0.6 copy.20
  152.8 16.7 %all-to-all-done.1 = f32[4,64,1,4,4]{3,4,0,2,1:T(4,128)S(1)} async-done(((f32[4,64,1,4,4]{3,4,0,2,1:T(4,128)}), f32[4,64,1,4,4]{3,4,0,2,1:T(4,128)S(1)}, u32[]{:S(2)}, u32[]{:S(2)}) %all-to-all-start.1) | async-done | bytes 16416 | tf_op jit(solution)/shard_map/all_to_all | solution.py:60
  169.5 0.9 copy.21
  (23 shorter events, 0.7 us)
Async XLA Ops:
  12.1 15.0 %copy-start.2 = (s32[4,2048]{1,0:T(4,128)S(1)}, s32[4,2048]{1,0:T(4,128)}, u32[]{:S(2)}) copy-start(s32[4,2048]{1,0:T(4,128)} %param.8) | copy-start | bytes 98308
  12.1 15.0 %copy-start.1 = (bf16[32,2048]{1,0:T(8,128)(2,1)S(1)}, bf16[32,2048]{1,0:T(8,128)(2,1)}, u32[]{:S(2)}) copy-start(bf16[32,2048]{1,0:T(8,128)(2,1)} %param.5) | copy-start | bytes 393220
  12.1 66.2 %all-to-all-start = ((bf16[64,8,2048]{2,1,0:T(8,128)(2,1)}), bf16[64,8,2048]{2,1,0:T(8,128)(2,1)S(1)}, u32[]{:S(2)}, u32[]{:S(2)}) async-start(bf16[64,8,2048]{2,1,0:T(8,128)(2,1)} %fusion.2), calls=%async_computation | async-start | bytes 4194304 | tf_op jit(solution)/shard_map/all_to_all | solution.py:35
  27.0 100.3 %reduce-scatter.2.cloned.1.call-start = ((), (), s32[]{:S(2)}) async-start(), calls=%async_computation.3 | async-start | bytes 884736 | tf_op jit(solution)/shard_map/reduce_scatter | solution.py:56
  90.5 2.1 %copy-start = (bf16[256,2048]{1,0:T(8,128)(2,1)S(1)}, bf16[256,2048]{1,0:T(8,128)(2,1)}, u32[]{:S(2)}) copy-start(bf16[256,2048]{1,0:T(8,128)(2,1)} %reshape.60) | copy-start | bytes 3145732
  136.4 33.1 %all-to-all-start.1 = ((f32[4,64,1,4,4]{3,4,0,2,1:T(4,128)}), f32[4,64,1,4,4]{3,4,0,2,1:T(4,128)S(1)}, u32[]{:S(2)}, u32[]{:S(2)}) async-start(f32[4,64,1,4,4]{3,4,0,2,1:T(4,128)} %copy.19), calls=%async_computation.2 | async-start | bytes 1048576 | tf_op jit(solution)/shard_map/all_to_all | solution.py:60
Sparse Core Ops, SparseCore 0:
  94.9 32.3 reduce-scatter.1

commit v2 on v1

v2 whole, which is shorter than its diff:
```python
import functools

import jax
import jax.numpy as jnp
from jax import lax
from jax.experimental import pallas as pl
from jax.experimental.pallas import tpu as pltpu
from jax.sharding import PartitionSpec as P

SUB = 4
NOPS = 4
MESH = pl.DeviceIdType.MESH


def gram(left, right):
    return lax.dot_general(
        left, right, (((1,), (1,)), ((), ())), preferred_element_type=jnp.float32
    )


def sums_kernel(left_ref, got_ref, out_ref):
    shares, _, cols = out_ref.shape
    groups = cols // SUB
    rows = got_ref.shape[0]
    got = got_ref[...]
    at = lax.broadcasted_iota(jnp.int32, (cols, rows), 0)
    source = lax.broadcasted_iota(jnp.int32, (cols, rows), 1)
    wanted = (at % groups) * (2 * SUB) + at // groups
    pick_x = (source == wanted).astype(jnp.float32).astype(jnp.bfloat16)
    pick_w = (source == wanted + SUB).astype(jnp.float32).astype(jnp.bfloat16)
    got_x = jnp.dot(pick_x, got, preferred_element_type=jnp.float32)
    got_w = jnp.dot(pick_w, got, preferred_element_type=jnp.float32)
    right_w = got_w.astype(jnp.bfloat16)
    wy = got_w * got_x
    right_wy = wy.astype(jnp.bfloat16)
    right_wyy = (wy * got_x).astype(jnp.bfloat16)
    left_w = left_ref[0]
    left_wx = left_ref[1]
    left_wxx = left_ref[2]
    parts = (
        gram(left_w, right_w),
        gram(left_wx, right_w),
        gram(left_wxx, right_w),
        gram(left_w, right_wy),
        gram(left_wx, right_wy),
        gram(left_w, right_wyy),
    )

    @pl.when(pl.program_id(0) == 0)
    def _():
        out_ref[...] = jnp.zeros_like(out_ref)

    for i, part in enumerate(parts):
        n = part.shape[0] // shares
        out_ref[:, i * n : (i + 1) * n, :] += part.reshape(shares, n, cols)


def six_sums(left, got, shares):
    width = left.shape[-1]
    rows = got.shape[0]
    tile = 512
    n = left.shape[1]
    return pl.pallas_call(
        sums_kernel,
        grid=(width // tile,),
        in_specs=[
            pl.BlockSpec((3, n, tile), lambda i: (0, 0, i)),
            pl.BlockSpec((rows, tile), lambda i: (0, i)),
        ],
        out_specs=pl.BlockSpec((shares, 6 * n // shares, rows // 2), lambda i: (0, 0, 0)),
        out_shape=jax.ShapeDtypeStruct((shares, 6 * n // shares, rows // 2), jnp.float32),
        compiler_params=pltpu.CompilerParams(vmem_limit_bytes=48 * 1024 * 1024),
    )(left, got)


def pearson(total_w, sum_x, sum_xx, sum_y, sum_xy, sum_yy):
    numer = total_w * sum_xy - sum_x * sum_y
    var_x = jnp.maximum(total_w * sum_xx - sum_x * sum_x, 0.05 * total_w * sum_xx)
    var_y = jnp.maximum(total_w * sum_yy - sum_y * sum_y, 0.05 * total_w * sum_yy)
    return numer / jnp.sqrt(var_x * var_y)


def finish_kernel(
    shares, groups, stats_ref, corr_ref, back_ref,
    held, msgs, landed, send_sem, recv_sem, out_sem, in_sem, own_sem,
):
    me_r = lax.axis_index("refl")
    me_d = lax.axis_index("dp")
    barrier = pltpu.get_barrier_semaphore()
    for t in range(1, shares):
        pl.semaphore_signal(
            barrier, inc=1, device_id={"refl": lax.rem(me_r + t, shares)}, device_id_type=MESH
        )

    @pl.loop(1, groups)
    def _(t):
        pl.semaphore_signal(
            barrier, inc=1, device_id={"dp": lax.rem(me_d + t, groups)}, device_id_type=MESH
        )

    pl.semaphore_wait(barrier, shares - 1 + groups - 1)
    copies = []
    for t in (4, 3, 5, 2, 6, 1, 7) if shares == 8 else range(1, shares):
        to = lax.rem(me_r + t, shares)
        copy = pltpu.make_async_remote_copy(
            src_ref=stats_ref.at[to],
            dst_ref=held.at[t - 1],
            send_sem=send_sem.at[t - 1],
            recv_sem=recv_sem.at[t - 1],
            device_id={"refl": to},
            device_id_type=MESH,
        )
        copy.start()
        copies.append((t, copy))
    total = stats_ref[me_r]
    for t, copy in sorted(copies, key=lambda c: min(c[0], shares - c[0])):
        copy.wait_recv()
        total = total + held[t - 1]
    n = total.shape[0] // 6
    corr = pearson(*[total[i * n : (i + 1) * n] for i in range(6)])
    corr_ref[...] = corr
    flipped = corr.T
    lined = jnp.concatenate(
        [flipped[u * groups : (u + 1) * groups] for u in range(SUB)]
        + [jnp.zeros((groups, 128 - SUB * n), jnp.float32)],
        1,
    )
    for s in range(groups):
        msgs[s] = lined[s : s + 1]
    own = pltpu.make_async_copy(msgs.at[me_d], landed.at[me_d], own_sem)
    own.start()

    @pl.loop(1, groups)
    def _(t):
        to = lax.rem(me_d + t, groups)
        pltpu.make_async_remote_copy(
            src_ref=msgs.at[to],
            dst_ref=landed.at[me_d],
            send_sem=out_sem,
            recv_sem=in_sem,
            device_id={"dp": to},
            device_id_type=MESH,
        ).start()

    for _, copy in copies:
        copy.wait_send()
    own.wait()
    some = pl.ds(0, groups - 1)
    pltpu.make_async_copy(msgs.at[some], msgs.at[some], out_sem).wait()
    pltpu.make_async_copy(landed.at[some], landed.at[some], in_sem).wait()
    back_ref[...] = landed[...]


def finish(stats, groups):
    shares, six, cols = stats.shape
    n = six // 6
    return pl.pallas_call(
        functools.partial(finish_kernel, shares, groups),
        out_shape=(
            jax.ShapeDtypeStruct((n, cols), jnp.float32),
            jax.ShapeDtypeStruct((groups, 1, 128), jnp.float32),
        ),
        in_specs=[pl.BlockSpec(memory_space=pltpu.VMEM)],
        out_specs=[pl.BlockSpec(memory_space=pltpu.VMEM)] * 2,
        scratch_shapes=[
            pltpu.VMEM((shares - 1, six, cols), jnp.float32),
            pltpu.VMEM((groups, 1, 128), jnp.float32),
            pltpu.VMEM((groups, 1, 128), jnp.float32),
            pltpu.SemaphoreType.DMA((shares - 1,)),
            pltpu.SemaphoreType.DMA((shares - 1,)),
            pltpu.SemaphoreType.DMA,
            pltpu.SemaphoreType.DMA,
            pltpu.SemaphoreType.DMA,
        ],
        compiler_params=pltpu.CompilerParams(collective_id=0, has_side_effects=True),
    )(stats)


def shards(intensities, observed, qweights, ops, pick):
    blk, width = intensities.shape
    groups = lax.axis_size("dp")
    shares = lax.axis_size("refl")
    rows = blk // shares
    own_w = (observed.astype(jnp.float32) * qweights.astype(jnp.float32)).astype(jnp.bfloat16)
    both = jnp.concatenate([intensities, own_w], 0)
    request = pick[:, 0][:, None] * SUB + jnp.arange(SUB, dtype=jnp.int32)[None, :]
    request = jnp.concatenate([request, request + blk], 1).reshape(-1)
    chosen = (request[:, None] == jnp.arange(2 * blk, dtype=jnp.int32)[None, :]).astype(jnp.bfloat16)
    send = jnp.dot(chosen, both, preferred_element_type=jnp.float32).astype(jnp.bfloat16)
    send = send.reshape(groups, 2 * SUB, width)
    got = lax.all_to_all(send, "dp", split_axis=0, concat_axis=0, tiled=True)
    local_ops = ops - lax.axis_index("refl") * width
    place = (local_ops[:, None, :] == jnp.arange(width, dtype=jnp.int32)[None, :, None]).astype(jnp.bfloat16)
    moved = jnp.einsum("ih,kgh->kig", both, place, preferred_element_type=jnp.float32)
    moved = moved.reshape(NOPS, 2, shares, rows, width).transpose(1, 2, 0, 3, 4)
    moved = moved.reshape(2, NOPS * blk, width)
    moved_x, moved_w = moved[0], moved[1]
    moved_wx = moved_w * moved_x
    left = jnp.stack([moved_w, moved_wx, moved_wx * moved_x], 0).astype(jnp.bfloat16)
    stats = six_sums(left, got.reshape(groups * 2 * SUB, width), shares)
    corr, back = finish(stats, groups)
    corr = corr.reshape(NOPS, rows, SUB, groups).transpose(0, 1, 3, 2)
    corr = corr.reshape(NOPS, rows, groups * SUB)
    back = back[:, 0, : SUB * NOPS * rows].reshape(groups, SUB, NOPS, rows)
    returned = back.transpose(2, 0, 1, 3)[:, None]
    return (corr, returned)


def solution(mesh):
    return jax.shard_map(
        shards,
        mesh=mesh,
        in_specs=(
            P("dp", "refl"),
            P("dp", "refl"),
            P("dp", "refl"),
            P(None, "refl"),
            P(None, "dp"),
        ),
        out_specs=(P(None, ("dp", "refl"), None), P(None, "dp", None, None, "refl")),
        check_vma=False,
    )
```

time: 178 us -> 118 us (0.66)
  waiting for transfers between devices: 85.5 us -> 23.6 us
  Pallas kernels: 0 us -> 39.9 us
  starting transfers between devices: 30.8 us -> 15 us
  between operations: 14.3 us -> 0.72 us
  other arithmetic: 10.2 us -> 4.53 us
  matrix products: 21 us -> 17.6 us
    pallas_call x0 -> x2, Pallas kernels: none -> 39.9 us  [the longest x1 35.2 us: finish(): pl.pallas_call(functools.partial(finish_kernel, shares, groups), out_shap...]
    reduce_scatter x1 -> x0, waiting for transfers between devices: 32.5 us -> none  [shards(): share = lax.psum_scatter(stats, 'refl', scatter_dimension=1, tiled=False)]
    all_to_all x1 -> x0, waiting for transfers between devices: 16.7 us -> none  [shards(): lax.all_to_all(outgoing, 'dp', split_axis=1, concat_axis=2, tiled=True)]
    all_to_all x1 -> x0, starting transfers between devices: 15.8 us -> none  [shards(): lax.all_to_all(outgoing, 'dp', split_axis=1, concat_axis=2, tiled=True)]
    all_to_all x1, waiting for transfers between devices: 36.3 us -> 23.6 us  [shards(): got = lax.all_to_all(send, 'dp', split_axis=0, concat_axis=0, tiled=True)]
    dot_general x3 -> x0, matrix products: 4.35 us -> none  [gram(): lax.dot_general(left, right, (((1,), (1,)), ((), ())), preferred_element_...]
    convert_element_type x2 -> x0, local copies, waits for them, and re-layouts: 4.11 us -> none  [the longest x1 2.14 us: shards(): right_wyy = (wide_w * got_x * got_x).astype(jnp.bfloat16)]
    slice x5 -> x3, local copies, waits for them, and re-layouts: 0.09 us -> 3.88 us  [the longest x2 3.05 us: shards(): moved_x, moved_w = (moved[0], moved[1])]
  transfers between devices with their start and end apart: 3 -> 1, of which waited for: 3 -> 1; matrix products, arithmetic and copies ran while one was open for 9% -> 23% of each run, Pallas kernels for 0% -> 0%
where the time goes in v2:
time: 118 us; the launch traced here: 117 us
  Pallas kernels  39.9 us (34%)
  waiting for transfers between devices  23.6 us (20%)
  matrix products  17.6 us (15%)
  local copies, waits for them, and re-layouts  16.1 us (14%)
  starting transfers between devices  15 us (13%)
  other arithmetic  4.53 us (4%)
    pallas_call x1, Pallas kernels, finish(): pl.pallas_call(functools.partial(finish_kernel, shares, groups), out_shap...  35.2 us
    all_to_all x1, waiting for transfers between devices, shards(): got = lax.all_to_all(send, 'dp', split_axis=0, concat_axis=0, tiled=True)  23.6 us
    all_to_all x1, starting transfers between devices, shards(): got = lax.all_to_all(send, 'dp', split_axis=0, concat_axis=0, tiled=True)  15 us
    dot_general x1, matrix products, shards(): jnp.einsum('ih,kgh->kig', both, place, preferred_element_type=jnp.float32)  14.6 us
    pallas_call x1, Pallas kernels, six_sums(): pl.pallas_call(sums_kernel, grid=(width // tile,), in_specs=[pl.BlockSpec...  4.73 us
    reshape x2, local copies, waits for them, and re-layouts, shards(): moved = moved.reshape(NOPS, 2, shares, rows, width).transpose(1, 2, 0, 3, 4)  4.57 us
    slice x2, local copies, waits for them, and re-layouts, shards(): moved_x, moved_w = (moved[0], moved[1])  3.05 us
    dot_general x1, matrix products, shards(): jnp.dot(chosen, both, preferred_element_type=jnp.float32)  3 us
  transfers between devices with their start and end apart: 1, of which 1 were waited for; matrix products, arithmetic and copies ran while one was open for 23% of the time, Pallas kernels for 0%

profile of v2, /device:TPU:1, one launch (start us, length us, event | category | flops | bytes accessed | tf_op | source)
XLA Modules:
  0.0 117.4 jit_solution(150786493557174247)
XLA Ops:
  0.6 0.7 multiply_bitcast_fusion
  1.3 0.1 copy.15
  1.4 0.1 eq.31
  1.5 1.1 multiply_convert_fusion.2
  2.5 3.0 %fusion.2 = bf16[64,8,2048]{2,1,0:T(8,128)(2,1)} fusion(bf16[32,2048]{1,0:T(8,128)(2,1)S(1)} %multiply_convert_fusion.2, bf16[32,2048]{1,0:T(8,128)(2,1)} %param.5, s32[512]{0:T(512)S(1)} %eq.31), kind=kOutput, calls=%fused_computation.4 | convolution fusion | flops 135823360 | bytes 2361344 | tf_op jit(solution)/shard_map/dot_general | solution.py:189
  5.5 0.0 copy-start.3
  5.5 0.0 copy-start.2
  5.5 15.0 %all-to-all-start = ((bf16[64,8,2048]{2,1,0:T(8,128)(2,1)}), bf16[64,8,2048]{2,1,0:T(8,128)(2,1)S(1)}, u32[]{:S(2)}, u32[]{:S(2)}) async-start(bf16[64,8,2048]{2,1,0:T(8,128)(2,1)} %fusion.2), calls=%async_computation | async-start | bytes 4194304 | tf_op jit(solution)/shard_map/all_to_all | solution.py:191
  20.5 0.0 copy-done.3
  20.5 0.0 copy-done.2
  20.6 14.6 %fusion.3 = f32[4,64,2048]{2,1,0:T(8,128)} fusion(s32[4,2048]{1,0:T(4,128)S(1)} %broadcast_subtract_fusion, bf16[32,2048]{1,0:T(8,128)(2,1)S(1)} %multiply_convert_fusion.2, bf16[32,2048]{1,0:T(8,128)(2,1)S(1)} %copy-done.2), kind=kOutput, calls=%fused_computation.5 | convolution fusion | flops 2164785152 | bytes 2392064 | tf_op jit(solution)/shard_map/ih,kgh->kig/dot_general | solution.py:194
  35.1 2.8 %reshape.60 = f32[4,2,8,4,2048]{4,3,2,1,0:T(4,128)} reshape(f32[4,64,2048]{2,1,0:T(8,128)} %fusion.3) | data formatting | bytes 4194304 | tf_op jit(solution)/shard_map/reshape | solution.py:195
  38.0 1.7 %copy.20 = f32[4,2,8,4,2048]{4,3,0,2,1:T(4,128)S(1)} copy(f32[4,2,8,4,2048]{4,3,2,1,0:T(4,128)} %reshape.60) | data formatting | bytes 4194304 | tf_op jit(solution)/shard_map/reshape | solution.py:195
  39.7 1.5 %fusion.8 = (f32[1,8,4,4,2048]{4,3,2,1,0:T(4,128)}, f32[1,8,4,4,2048]{4,3,2,1,0:T(4,128)}) fusion(f32[2,8,4,4,2048]{4,3,2,1,0:T(4,128)S(1)} %bitcast.23), kind=kLoop, calls=%fused_computation.22 | loop fusion | bytes 4194304 | tf_op jit(solution)/shard_map/slice | solution.py:197
  41.2 1.6 %slice.14 = f32[1,128,2048]{2,1,0:T(8,128)S(1)} reshape(f32[1,8,4,4,2048]{4,3,2,1,0:T(4,128)} %get-tuple-element.12) | data formatting | bytes 2097152 | tf_op jit(solution)/shard_map/slice | solution.py:197
  42.8 2.6 %squeeze.4 = f32[1,128,2048]{2,1,0:T(8,128)} reshape(f32[1,8,4,4,2048]{4,3,2,1,0:T(4,128)} %get-tuple-element.13) | data formatting | bytes 2097152 | tf_op jit(solution)/shard_map/squeeze | solution.py:197
  45.3 1.5 %multiply_convert_fusion.1 = (bf16[1,128,2048]{2,1,0:T(8,128)(2,1)S(1)}, bf16[1,128,2048]{2,1,0:T(8,128)(2,1)S(1)}, bf16[1,128,2048]{2,1,0:T(8,128)(2,1)S(1)}) fusion(f32[1,128,2048]{2,1,0:T(8,128)S(1)} %slice.14, f32[1,128,2048]{2,1,0:T(8,128)} %squeeze.4), kind=kLoop, calls=%fused_computation.9 | loop fusion | flops 1310720 | bytes 3670016 | tf_op jit(solution)/shard_map/convert.1
  46.8 1.3 %pad_maximum_fusion.left_ref = bf16[3,128,2048]{2,1,0:T(8,128)(2,1)} fusion(bf16[1,128,2048]{2,1,0:T(8,128)(2,1)S(1)} %get-tuple-element.11, bf16[1,128,2048]{2,1,0:T(8,128)(2,1)S(1)} %get-tuple-element.10, bf16[1,128,2048]{2,1,0:T(8,128)(2,1)S(1)} %get-tuple-element.14), kind=kLoop, calls=%fused_computation.7 | loop fusion | flops 1572864 | bytes 3145728 | tf_op jit(solution)/shard_map/stack | solution.py:199
  48.1 23.6 %all-to-all-done = bf16[64,8,2048]{2,1,0:T(8,128)(2,1)S(1)} async-done(((bf16[64,8,2048]{2,1,0:T(8,128)(2,1)}), bf16[64,8,2048]{2,1,0:T(8,128)(2,1)S(1)}, u32[]{:S(2)}, u32[]{:S(2)}) %all-to-all-start) | async-done | bytes 2097184 | tf_op jit(solution)/shard_map/all_to_all | solution.py:191
  71.7 0.0 copy-start
  71.7 1.4 %copy-done = bf16[3,128,2048]{2,1,0:T(8,128)(2,1)S(1)} copy-done((bf16[3,128,2048]{2,1,0:T(8,128)(2,1)S(1)}, bf16[3,128,2048]{2,1,0:T(8,128)(2,1)}, u32[]{:S(2)}) %copy-start) | copy-done | bytes 1572888
  73.1 4.7 %shard_map.68.stats_ref = f32[8,96,256]{2,1,0:T(8,128)S(1)} custom-call(bf16[3,128,2048]{2,1,0:T(8,128)(2,1)S(1)} %copy-done, bf16[512,2048]{1,0:T(8,128)(2,1)S(1)} %bitcast.22), custom_call_target="tpu_custom_call" | custom-call | tf_op jit(solution)/shard_map/pallas_call | solution.py:63
  77.9 0.0 copy-start.1
  77.9 0.9 copy-done.1
  78.7 35.2 %shard_map.69 = (f32[16,256]{1,0:T(8,128)}, f32[64,1,128]{2,1,0:T(1,128)}) custom-call(f32[8,96,256]{2,1,0:T(8,128)} %copy-done.1), custom_call_target="tpu_custom_call" | custom-call | tf_op jit(solution)/shard_map/pallas_call | solution.py:157
  114.0 0.8 copy.17
  114.8 0.6 copy.18
  115.4 0.8 reshape.63
  116.2 0.2 copy.16
  116.5 0.9 reshape.64
  (3 shorter events, 0.0 us)
Async XLA Ops:
  5.5 15.0 %copy-start.3 = (s32[4,2048]{1,0:T(4,128)S(1)}, s32[4,2048]{1,0:T(4,128)}, u32[]{:S(2)}) copy-start(s32[4,2048]{1,0:T(4,128)} %param.8) | copy-start | bytes 98308
  5.5 15.0 %copy-start.2 = (bf16[32,2048]{1,0:T(8,128)(2,1)S(1)}, bf16[32,2048]{1,0:T(8,128)(2,1)}, u32[]{:S(2)}) copy-start(bf16[32,2048]{1,0:T(8,128)(2,1)} %param.5) | copy-start | bytes 393220
  5.5 66.2 %all-to-all-start = ((bf16[64,8,2048]{2,1,0:T(8,128)(2,1)}), bf16[64,8,2048]{2,1,0:T(8,128)(2,1)S(1)}, u32[]{:S(2)}, u32[]{:S(2)}) async-start(bf16[64,8,2048]{2,1,0:T(8,128)(2,1)} %fusion.2), calls=%async_computation | async-start | bytes 4194304 | tf_op jit(solution)/shard_map/all_to_all | solution.py:191
  71.7 1.4 %copy-start = (bf16[3,128,2048]{2,1,0:T(8,128)(2,1)S(1)}, bf16[3,128,2048]{2,1,0:T(8,128)(2,1)}, u32[]{:S(2)}) copy-start(bf16[3,128,2048]{2,1,0:T(8,128)(2,1)} %pad_maximum_fusion.left_ref) | copy-start | bytes 4718596
  77.9 0.9 copy-start.1

commit v3 on v1

v3 whole, which is shorter than its diff:
```python
import functools

import jax
import jax.numpy as jnp
from jax import lax
from jax.experimental import pallas as pl
from jax.experimental.pallas import tpu as pltpu
from jax.sharding import PartitionSpec as P

SUB = 4
NOPS = 4
MESH = pl.DeviceIdType.MESH


def gram(left, right):
    return lax.dot_general(
        left, right, (((1,), (1,)), ((), ())), preferred_element_type=jnp.float32
    )


def pearson(total_w, sum_x, sum_xx, sum_y, sum_xy, sum_yy):
    numer = total_w * sum_xy - sum_x * sum_y
    var_x = jnp.maximum(total_w * sum_xx - sum_x * sum_x, 0.05 * total_w * sum_xx)
    var_y = jnp.maximum(total_w * sum_yy - sum_y * sum_y, 0.05 * total_w * sum_yy)
    return numer / jnp.sqrt(var_x * var_y)


def whole_kernel(
    shares, groups, send_ref, both_ref, ops_ref, corr_ref, back_ref,
    landed, moved, left, stats, held, msgs, returned,
    send_sem, recv_sem, own_sem, part_send, part_recv, out_sem, in_sem, kept_sem,
):
    me_r = lax.axis_index("refl")
    me_d = lax.axis_index("dp")
    half = groups // 2
    me_s = me_d // 2
    me_c = lax.rem(me_d, 2)
    cores = (me_c, 1 - me_c)
    width = both_ref.shape[1]
    blk = both_ref.shape[0] // 2
    rows = blk // shares
    n = NOPS * rows
    barrier = pltpu.get_barrier_semaphore()
    for t in range(1, shares):
        pl.semaphore_signal(
            barrier, inc=1, device_id={"refl": lax.rem(me_r + t, shares)}, device_id_type=MESH
        )

    @pl.loop(1, groups)
    def _(t):
        pl.semaphore_signal(
            barrier, inc=1, device_id={"dp": lax.rem(me_d + t, groups)}, device_id_type=MESH
        )

    pl.semaphore_wait(barrier, shares - 1 + groups - 1)
    own = pltpu.make_async_copy(send_ref.at[me_d], landed.at[0, me_s], own_sem)
    own.start()
    for p in range(2):

        @pl.loop(1 - p, half)
        def _(t):
            to = lax.rem(me_s + t, half) * 2 + cores[p]
            pltpu.make_async_remote_copy(
                src_ref=send_ref.at[to],
                dst_ref=landed.at[p, me_s],
                send_sem=send_sem.at[p],
                recv_sem=recv_sem.at[p],
                device_id={"dp": to},
                device_id_type=MESH,
            ).start()

    both = both_ref[...]
    step = 256
    for k in range(NOPS):
        line = ops_ref[k : k + 1, :] - me_r * width

        @pl.loop(0, width // step)
        def _(g):
            at = lax.broadcasted_iota(jnp.int32, (step, width), 0) + g * step
            place = (at == line).astype(jnp.float32).astype(jnp.bfloat16)
            lanes = pl.ds(pl.multiple_of(g * step, step), step)
            put = gram(both, place).astype(jnp.bfloat16)
            moved[0, k * blk : (k + 1) * blk, lanes] = put[:blk]
            moved[1, k * blk : (k + 1) * blk, lanes] = put[blk:]

    to_row = lax.broadcasted_iota(jnp.int32, (NOPS * blk, NOPS * blk), 0)
    from_row = lax.broadcasted_iota(jnp.int32, (NOPS * blk, NOPS * blk), 1)
    want = ((to_row // rows) % NOPS) * blk + (to_row // n) * rows + to_row % rows
    order = (from_row == want).astype(jnp.float32).astype(jnp.bfloat16)
    tile = 512

    @pl.loop(0, width // tile)
    def _(g):
        lanes = pl.ds(pl.multiple_of(g * tile, tile), tile)
        own_x = jnp.dot(order, moved[0, :, lanes], preferred_element_type=jnp.float32)
        own_w = jnp.dot(order, moved[1, :, lanes], preferred_element_type=jnp.float32)
        own_wx = own_w * own_x
        left[0, :, lanes] = own_w.astype(jnp.bfloat16)
        left[1, :, lanes] = own_wx.astype(jnp.bfloat16)
        left[2, :, lanes] = (own_wx * own_x).astype(jnp.bfloat16)

    cols = half * SUB
    height = half * 2 * SUB
    at = lax.broadcasted_iota(jnp.int32, (cols, height), 0)
    source = lax.broadcasted_iota(jnp.int32, (cols, height), 1)
    wanted = (at % half) * (2 * SUB) + at // half
    pick_x = (source == wanted).astype(jnp.float32).astype(jnp.bfloat16)
    pick_w = (source == wanted + SUB).astype(jnp.float32).astype(jnp.bfloat16)
    copies = [[], []]
    for p in range(2):
        if p == 0:
            own.wait()
            some = pl.ds(0, half - 1)
            pltpu.make_async_copy(landed.at[0, some], landed.at[0, some], recv_sem.at[0]).wait()
        else:
            pltpu.make_async_copy(landed.at[1], landed.at[1], recv_sem.at[1]).wait()
        stats[p] = jnp.zeros(stats.shape[1:], jnp.float32)

        @pl.loop(0, width // tile)
        def _(g):
            lanes = pl.ds(pl.multiple_of(g * tile, tile), tile)
            got = landed[p, :, :, lanes].astype(jnp.float32).reshape(height, tile).astype(jnp.bfloat16)
            got_x = jnp.dot(pick_x, got, preferred_element_type=jnp.float32)
            got_w = jnp.dot(pick_w, got, preferred_element_type=jnp.float32)
            right_w = got_w.astype(jnp.bfloat16)
            wy = got_w * got_x
            right_wy = wy.astype(jnp.bfloat16)
            right_wyy = (wy * got_x).astype(jnp.bfloat16)
            left_w = left[0, :, lanes]
            left_wx = left[1, :, lanes]
            left_wxx = left[2, :, lanes]
            parts = (
                gram(left_w, right_w),
                gram(left_wx, right_w),
                gram(left_wxx, right_w),
                gram(left_w, right_wy),
                gram(left_wx, right_wy),
                gram(left_w, right_wyy),
            )
            for i, part in enumerate(parts):
                stats[p, :, i * n : (i + 1) * n, :] += part.reshape(shares, n, cols)

        for t in (4, 3, 5, 2, 6, 1, 7) if shares == 8 else range(1, shares):
            to = lax.rem(me_r + t, shares)
            copy = pltpu.make_async_remote_copy(
                src_ref=stats.at[p, to],
                dst_ref=held.at[p, t - 1],
                send_sem=part_send.at[p, t - 1],
                recv_sem=part_recv.at[p, t - 1],
                device_id={"refl": to},
                device_id_type=MESH,
            )
            copy.start()
            copies[p].append((t, copy))
    kept = pltpu.make_async_copy(msgs.at[0, me_s], returned.at[me_c, me_s], kept_sem)
    for p in range(2):
        total = stats[p, me_r]
        for t, copy in sorted(copies[p], key=lambda c: min(c[0], shares - c[0])):
            copy.wait_recv()
            total = total + held[p, t - 1]
        corr = pearson(*[total[i * n : (i + 1) * n] for i in range(6)])
        corr_ref[cores[p]] = corr
        flipped = corr.T
        lined = jnp.concatenate(
            [flipped[u * half : (u + 1) * half] for u in range(SUB)]
            + [jnp.zeros((half, 128 - SUB * n), jnp.float32)],
            1,
        )
        for s in range(half):
            msgs[p, s] = lined[s : s + 1]
        if p == 0:
            kept.start()

        @pl.loop(1 - p, half)
        def _(t):
            to = lax.rem(me_s + t, half)
            pltpu.make_async_remote_copy(
                src_ref=msgs.at[p, to],
                dst_ref=returned.at[me_c, me_s],
                send_sem=out_sem.at[p],
                recv_sem=in_sem.at[p],
                device_id={"dp": to * 2 + cores[p]},
                device_id_type=MESH,
            ).start()

    kept.wait()
    for p in range(2):
        for _, copy in copies[p]:
            copy.wait_send()
        many = pl.ds(0, half - 1 + p)
        pltpu.make_async_copy(landed.at[p, many], landed.at[p, many], send_sem.at[p]).wait()
        pltpu.make_async_copy(msgs.at[p, many], msgs.at[p, many], out_sem.at[p]).wait()
        pltpu.make_async_copy(returned.at[p, many], returned.at[p, many], in_sem.at[p]).wait()
    back_ref[...] = returned[...]


def whole(send, both, ops, shares):
    groups, eight, width = send.shape
    half = groups // 2
    blk = both.shape[0] // 2
    n = NOPS * (blk // shares)
    cols = half * SUB
    vmem = pl.BlockSpec(memory_space=pltpu.VMEM)
    dma = pltpu.SemaphoreType.DMA
    return pl.pallas_call(
        functools.partial(whole_kernel, shares, groups),
        out_shape=(
            jax.ShapeDtypeStruct((2, n, cols), jnp.float32),
            jax.ShapeDtypeStruct((2, half, 1, 128), jnp.float32),
        ),
        in_specs=[pl.BlockSpec(memory_space=pl.ANY), vmem, vmem],
        out_specs=[vmem, vmem],
        scratch_shapes=[
            pltpu.VMEM((2, half, eight, width), jnp.bfloat16),
            pltpu.VMEM((2, NOPS * blk, width), jnp.bfloat16),
            pltpu.VMEM((3, NOPS * blk, width), jnp.bfloat16),
            pltpu.VMEM((2, shares, 6 * n, cols), jnp.float32),
            pltpu.VMEM((2, shares - 1, 6 * n, cols), jnp.float32),
            pltpu.VMEM((2, half, 1, 128), jnp.float32),
            pltpu.VMEM((2, half, 1, 128), jnp.float32),
            dma((2,)),
            dma((2,)),
            dma,
            dma((2, shares - 1)),
            dma((2, shares - 1)),
            dma((2,)),
            dma((2,)),
            dma,
        ],
        compiler_params=pltpu.CompilerParams(
            collective_id=0, has_side_effects=True, vmem_limit_bytes=48 * 1024 * 1024
        ),
    )(send, both, ops)


def shards(intensities, observed, qweights, ops, pick):
    blk, width = intensities.shape
    groups = lax.axis_size("dp")
    shares = lax.axis_size("refl")
    rows = blk // shares
    own_w = (observed.astype(jnp.float32) * qweights.astype(jnp.float32)).astype(jnp.bfloat16)
    both = jnp.concatenate([intensities, own_w], 0)
    request = pick[:, 0][:, None] * SUB + jnp.arange(SUB, dtype=jnp.int32)[None, :]
    request = jnp.concatenate([request, request + blk], 1).reshape(-1)
    chosen = (request[:, None] == jnp.arange(2 * blk, dtype=jnp.int32)[None, :]).astype(jnp.bfloat16)
    send = jnp.dot(chosen, both, preferred_element_type=jnp.float32).astype(jnp.bfloat16)
    send = send.reshape(groups, 2 * SUB, width)
    corr, back = whole(send, both, ops, shares)
    corr = corr.reshape(2, NOPS, rows, SUB, groups // 2).transpose(1, 2, 4, 0, 3)
    corr = corr.reshape(NOPS, rows, groups * SUB)
    back = back[:, :, 0, : SUB * NOPS * rows].reshape(2, groups // 2, SUB, NOPS, rows)
    returned = back.transpose(3, 1, 0, 2, 4).reshape(NOPS, 1, groups, SUB, rows)
    return (corr, returned)


def solution(mesh):
    return jax.shard_map(
        shards,
        mesh=mesh,
        in_specs=(
            P("dp", "refl"),
            P("dp", "refl"),
            P("dp", "refl"),
            P(None, "refl"),
            P(None, "dp"),
        ),
        out_specs=(P(None, ("dp", "refl"), None), P(None, "dp", None, None, "refl")),
        check_vma=False,
    )
```

time: 178 us -> 91.9 us (0.52)
  waiting for transfers between devices: 85.5 us -> 0 us
  Pallas kernels: 0 us -> 84.5 us
  starting transfers between devices: 30.8 us -> 0 us
  matrix products: 21 us -> 1.66 us
  between operations: 14.3 us -> 0.7 us
  local copies, waits for them, and re-layouts: 15.4 us -> 3.09 us
  other arithmetic: 10.2 us -> 1.79 us
    pallas_call x0 -> x1, Pallas kernels: none -> 84.5 us  [whole(): pl.pallas_call(functools.partial(whole_kernel, shares, groups), out_shape...]
    all_to_all x2 -> x0, waiting for transfers between devices: 53 us -> none  [the longest x1 36.3 us: shards(): got = lax.all_to_all(send, 'dp', split_axis=0, concat_axis=0, tiled=True)]
    reduce_scatter x1 -> x0, waiting for transfers between devices: 32.5 us -> none  [shards(): share = lax.psum_scatter(stats, 'refl', scatter_dimension=1, tiled=False)]
    all_to_all x2 -> x0, starting transfers between devices: 30.8 us -> none  [the longest x1 15.8 us: shards(): lax.all_to_all(outgoing, 'dp', split_axis=1, concat_axis=2, tiled=True)]
    dot_general x4 -> x0, matrix products: 18 us -> none  [the longest x1 13.7 us: shards(): jnp.einsum('ih,kgh->kig', both, place, preferred_element_type=jnp.float32)]
    convert_element_type x2 -> x0, local copies, waits for them, and re-layouts: 4.11 us -> none  [the longest x1 2.14 us: shards(): right_wyy = (wide_w * got_x * got_x).astype(jnp.bfloat16)]
    slice x2 -> x0, other arithmetic: 3.32 us -> none  [the longest x1 2.45 us: shards(): got_w = got[:, SUB:].reshape(groups * SUB, width)]
    squeeze x4 -> x0, local copies, waits for them, and re-layouts: 2.97 us -> none  [shards(): corr = pearson(*[share[i] for i in range(6)])]
  transfers between devices with their start and end apart: 3 -> 0, of which waited for: 3 -> 0; matrix products, arithmetic and copies ran while one was open for 9% -> 0% of each run, Pallas kernels for 0% -> 0%
where the time goes in v3:
time: 91.9 us; the launch traced here: 91.7 us
  Pallas kernels  84.5 us (92%)
  local copies, waits for them, and re-layouts  3.09 us (3%)
  other arithmetic  1.79 us (2%)
  matrix products  1.66 us (2%)
    pallas_call x1, Pallas kernels, whole(): pl.pallas_call(functools.partial(whole_kernel, shares, groups), out_shape...  84.5 us

profile of v3, /device:TPU:1, one launch (start us, length us, event | category | flops | bytes accessed | tf_op | source)
XLA Modules:
  0.0 91.7 jit_solution(986238775401236815)
XLA Ops:
  0.6 0.0 copy-start.1
  0.6 0.0 copy-start
  0.7 0.7 multiply_bitcast_fusion
  1.4 0.1 copy.13
  1.5 0.1 eq.15
  1.5 1.1 %multiply_convert_fusion = bf16[32,2048]{1,0:T(8,128)(2,1)S(1)} fusion(bf16[32,2048]{1,0:T(8,128)(2,1)} %param.7, s32[32,2048]{1,0:T(8,128)} %param.6), kind=kLoop, calls=%fused_computation.3 | loop fusion | flops 262144 | bytes 524288 | tf_op jit(solution)/shard_map/convert_element_type | solution.py:241
  2.6 1.7 %fusion.send_ref = bf16[64,8,2048]{2,1,0:T(8,128)(2,1)S(1)} fusion(s32[512]{0:T(512)S(1)} %eq.15, bf16[32,2048]{1,0:T(8,128)(2,1)S(1)} %multiply_convert_fusion, bf16[32,2048]{1,0:T(8,128)(2,1)} %param.5), kind=kOutput, calls=%fused_computation.1 | convolution fusion | flops 135823360 | bytes 2361344 | tf_op jit(solution)/shard_map/dot_general | solution.py:246
  4.3 0.0 copy-done.1
  4.3 0.0 copy-done
  4.3 84.5 %shard_map.68 = (f32[2,16,128]{2,1,0:T(8,128)S(1)}, f32[2,32,1,128]{3,2,1,0:T(1,128)S(1)}) custom-call(bf16[64,8,2048]{2,1,0:T(8,128)(2,1)S(1)} %fusion.send_ref, bf16[64,2048]{1,0:T(8,128)(2,1)S(1)} %pad_maximum_fusion.both_ref, s32[4,2048]{1,0:T(4,128)S(1)} %copy-done), custom_call_target="tpu_custom_call" | custom-call | tf_op jit(solution)/shard_map/pallas_call | solution.py:205
  88.8 0.1 copy.15
  88.9 0.3 copy.16
  89.2 0.8 copy.17
  90.0 0.1 reshape.18
  90.1 0.3 copy.14
  90.4 1.3 %reshape.19 = f32[4,4,256]{2,1,0:T(4,128)} reshape(f32[4,4,32,2,4]{4,3,2,1,0:T(2,128)S(1)} %bitcast.12) | data formatting | bytes 32768 | tf_op jit(solution)/shard_map/reshape | solution.py:250
  (3 shorter events, 0.0 us)
Async XLA Ops:
  0.6 3.6 %copy-start.1 = (bf16[32,2048]{1,0:T(8,128)(2,1)S(1)}, bf16[32,2048]{1,0:T(8,128)(2,1)}, u32[]{:S(2)}) copy-start(bf16[32,2048]{1,0:T(8,128)(2,1)} %param.5) | copy-start | bytes 393220
  0.6 3.7 %copy-start = (s32[4,2048]{1,0:T(4,128)S(1)}, s32[4,2048]{1,0:T(4,128)}, u32[]{:S(2)}) copy-start(s32[4,2048]{1,0:T(4,128)} %ops_ref.1) | copy-start | bytes 98308

commit v4 on v3

v4 whole, which is shorter than its diff:
```python
import functools

import jax
import jax.numpy as jnp
from jax import lax
from jax.experimental import pallas as pl
from jax.experimental.pallas import tpu as pltpu
from jax.sharding import PartitionSpec as P

SUB = 4
NOPS = 4
MESH = pl.DeviceIdType.MESH


def gram(left, right):
    return lax.dot_general(
        left, right, (((1,), (1,)), ((), ())), preferred_element_type=jnp.float32
    )


def pearson(total_w, sum_x, sum_xx, sum_y, sum_xy, sum_yy):
    numer = total_w * sum_xy - sum_x * sum_y
    var_x = jnp.maximum(total_w * sum_xx - sum_x * sum_x, 0.05 * total_w * sum_xx)
    var_y = jnp.maximum(total_w * sum_yy - sum_y * sum_y, 0.05 * total_w * sum_yy)
    return numer / jnp.sqrt(var_x * var_y)


def whole_kernel(
    shares, groups, deep, block_ref, ops_ref, corr_ref, back_ref,
    ring, outbox, landed, moved, left, stats, held, msgs, returned,
    ring_send, ring_recv, send_sem, recv_sem, own_sem, part_send, part_recv, out_sem, in_sem, kept_sem,
):
    me_r = lax.axis_index("refl")
    me_d = lax.axis_index("dp")
    half = groups // 2
    tall = groups // deep
    quad = deep // 2
    me_c = lax.rem(me_d, 2)
    me_z = lax.rem(me_d // 2, deep)
    me_p = (me_d // (2 * deep)) * 2 + me_c
    width = block_ref.shape[2]
    blk = (block_ref.shape[0] - 1) * block_ref.shape[1] // 2
    rows = blk // shares
    n = NOPS * rows

    def device(p, z):
        return ((p // 2) * deep + z) * 2 + lax.rem(p, 2)

    barrier = pltpu.get_barrier_semaphore()
    for t in range(1, shares):
        pl.semaphore_signal(
            barrier, inc=1, device_id={"refl": lax.rem(me_r + t, shares)}, device_id_type=MESH
        )

    @pl.loop(1, groups)
    def _(t):
        pl.semaphore_signal(
            barrier, inc=1, device_id={"dp": lax.rem(me_d + t, groups)}, device_id_type=MESH
        )

    pl.semaphore_wait(barrier, shares - 1 + groups - 1)
    up = device(me_p, lax.rem(me_z + 1, deep))
    down = device(me_p, lax.rem(me_z + deep - 1, deep))
    far = quad - 1
    last = 2 * far
    cut = blk // 8
    tiles = 2 * cut + 1

    def hop(i, src, dst, to):
        copy = pltpu.make_async_remote_copy(
            src_ref=src,
            dst_ref=dst,
            send_sem=ring_send.at[i],
            recv_sem=ring_recv.at[i],
            device_id={"dp": to},
            device_id_type=MESH,
        )
        copy.start()
        return copy

    def hop_up(j):
        src = block_ref if j == 1 else ring.at[j - 2]
        if j <= far:
            return hop(j - 1, src, ring.at[j - 1], up)
        part = pl.ds(0, cut)
        return hop(j - 1, src.at[part], ring.at[last, part], up)

    def hop_down(j):
        src = block_ref if j == 1 else ring.at[far + j - 2]
        if j <= far:
            return hop(quad + j - 1, src, ring.at[far + j - 1], down)
        part = pl.ds(cut, tiles - cut)
        return hop(quad + j - 1, src.at[part], ring.at[last, part], down)

    row_at = lax.broadcasted_iota(jnp.int32, (tall * 8, 128), 0)
    lane_at = lax.broadcasted_iota(jnp.int32, (tall * 8, 128), 1)
    asks = lane_at == device(row_at // 8, me_z)
    row_in = (lax.rem(row_at // SUB, 2) * blk + lax.rem(row_at, SUB)).astype(jnp.float32)[:, : 2 * blk]
    lane_in = lane_at.astype(jnp.float32)[:, : 2 * blk]
    waiting = {}

    def rows_of(ref):
        return ref[: 2 * cut].astype(jnp.float32).reshape(2 * blk, width).astype(jnp.bfloat16)

    def serve(offset, ref):
        w = (offset + quad - 2) % deep
        p, q = w // quad, w % quad
        line = ref[2 * cut, :, :128].astype(jnp.float32)[0:1]
        asked = jnp.sum(jnp.where(asks, line, 0.0), axis=1, keepdims=True)
        chosen = (lane_in == row_in + asked * SUB).astype(jnp.float32).astype(jnp.bfloat16)
        got = jnp.dot(chosen, rows_of(ref), preferred_element_type=jnp.float32)
        outbox[w] = got.reshape(tall, 8, width).astype(jnp.bfloat16)
        own = pltpu.make_async_copy(
            outbox.at[w, me_p], landed.at[p, me_p * quad + q], own_sem.at[w]
        )
        own.start()
        waiting[w] = own

        @pl.loop(1, tall)
        def _(t):
            to = lax.rem(me_p + t, tall)
            pltpu.make_async_remote_copy(
                src_ref=outbox.at[w, to],
                dst_ref=landed.at[p, me_p * quad + q],
                send_sem=send_sem.at[p],
                recv_sem=recv_sem.at[p],
                device_id={"dp": device(to, me_z)},
                device_id_type=MESH,
            ).start()

    step = 256

    def operate(k):
        line = ops_ref[k : k + 1, :] - me_r * width
        both = rows_of(block_ref)

        @pl.loop(0, width // step)
        def _(g):
            at = lax.broadcasted_iota(jnp.int32, (step, width), 0) + g * step
            place = (at == line).astype(jnp.float32).astype(jnp.bfloat16)
            lanes = pl.ds(pl.multiple_of(g * step, step), step)
            put = gram(both, place).astype(jnp.bfloat16)
            moved[0, k * blk : (k + 1) * blk, lanes] = put[:blk]
            moved[1, k * blk : (k + 1) * blk, lanes] = put[blk:]

    tile = 512

    def weigh():
        to_row = lax.broadcasted_iota(jnp.int32, (NOPS * blk, NOPS * blk), 0)
        from_row = lax.broadcasted_iota(jnp.int32, (NOPS * blk, NOPS * blk), 1)
        want = ((to_row // rows) % NOPS) * blk + (to_row // n) * rows + to_row % rows
        order = (from_row == want).astype(jnp.float32).astype(jnp.bfloat16)

        @pl.loop(0, width // tile)
        def _(g):
            lanes = pl.ds(pl.multiple_of(g * tile, tile), tile)
            own_x = jnp.dot(order, moved[0, :, lanes], preferred_element_type=jnp.float32)
            own_w = jnp.dot(order, moved[1, :, lanes], preferred_element_type=jnp.float32)
            own_wx = own_w * own_x
            left[0, :, lanes] = own_w.astype(jnp.bfloat16)
            left[1, :, lanes] = own_wx.astype(jnp.bfloat16)
            left[2, :, lanes] = (own_wx * own_x).astype(jnp.bfloat16)

    cols = half * SUB
    height = half * 2 * SUB
    at = lax.broadcasted_iota(jnp.int32, (cols, height), 0)
    source = lax.broadcasted_iota(jnp.int32, (cols, height), 1)
    wanted = (at % half) * (2 * SUB) + at // half
    pick_x = (source == wanted).astype(jnp.float32).astype(jnp.bfloat16)
    pick_w = (source == wanted + SUB).astype(jnp.float32).astype(jnp.bfloat16)
    copies = [[], []]

    def sums(p):
        for w in range(p * quad, (p + 1) * quad):
            waiting[w].wait()
        many = pl.ds(0, quad * (tall - 1))
        pltpu.make_async_copy(landed.at[p, many], landed.at[p, many], recv_sem.at[p]).wait()
        stats[p] = jnp.zeros(stats.shape[1:], jnp.float32)

        @pl.loop(0, width // tile)
        def _(g):
            lanes = pl.ds(pl.multiple_of(g * tile, tile), tile)
            got = landed[p, :, :, lanes].astype(jnp.float32).reshape(height, tile).astype(jnp.bfloat16)
            got_x = jnp.dot(pick_x, got, preferred_element_type=jnp.float32)
            got_w = jnp.dot(pick_w, got, preferred_element_type=jnp.float32)
            right_w = got_w.astype(jnp.bfloat16)
            wy = got_w * got_x
            right_wy = wy.astype(jnp.bfloat16)
            right_wyy = (wy * got_x).astype(jnp.bfloat16)
            left_w = left[0, :, lanes]
            left_wx = left[1, :, lanes]
            left_wxx = left[2, :, lanes]
            parts = (
                gram(left_w, right_w),
                gram(left_wx, right_w),
                gram(left_wxx, right_w),
                gram(left_w, right_wy),
                gram(left_wx, right_wy),
                gram(left_w, right_wyy),
            )
            for i, part in enumerate(parts):
                stats[p, :, i * n : (i + 1) * n, :] += part.reshape(shares, n, cols)

        for t in (4, 3, 5, 2, 6, 1, 7) if shares == 8 else range(1, shares):
            to = lax.rem(me_r + t, shares)
            copy = pltpu.make_async_remote_copy(
                src_ref=stats.at[p, to],
                dst_ref=held.at[p, t - 1],
                send_sem=part_send.at[p, t - 1],
                recv_sem=part_recv.at[p, t - 1],
                device_id={"refl": to},
                device_id_type=MESH,
            )
            copy.start()
            copies[p].append((t, copy))
    hops = [hop_up(1), hop_down(1)]
    serve(0, block_ref)
    operate(0)
    operate(1)
    for j in range(1, quad):
        above, below = hops[-2:]
        above.wait_recv()
        hops.append(hop_up(j + 1))
        below.wait_recv()
        hops.append(hop_down(j + 1))
        serve(-j, ring.at[j - 1])
        serve(j, ring.at[far + j - 1])
        if j == 1:
            operate(2)
        elif j == 2:
            operate(3)
            weigh()
    sums(0)
    for copy in hops[-2:]:
        copy.wait_recv()
    serve(quad, ring.at[last])
    sums(1)
    kept = pltpu.make_async_copy(msgs.at[me_d], returned.at[me_d], kept_sem)
    for p in range(2):
        total = stats[p, me_r]
        for t, copy in sorted(copies[p], key=lambda c: min(c[0], shares - c[0])):
            copy.wait_recv()
            total = total + held[p, t - 1]
        corr = pearson(*[total[i * n : (i + 1) * n] for i in range(6)])
        flipped = corr.T
        lined = jnp.concatenate(
            [flipped[u * half : (u + 1) * half] for u in range(SUB)]
            + [jnp.zeros((half, 128 - SUB * n), jnp.float32)],
            1,
        )
        for i in range(half):
            z = lax.rem(me_z + p * quad + i % quad - (quad - 2) + deep, deep)
            msgs[device(i // quad, z)] = lined[i : i + 1]
        if p == 0:
            kept.start()

        @pl.loop(0, quad)
        def _(q):
            z = lax.rem(me_z + p * quad + q - (quad - 2) + deep, deep)

            @pl.loop(0, tall)
            def _(t):
                to = device(lax.rem(me_p + t, tall), z)

                @pl.when(to != me_d)
                def _():
                    pltpu.make_async_remote_copy(
                        src_ref=msgs.at[to],
                        dst_ref=returned.at[me_d],
                        send_sem=out_sem.at[p],
                        recv_sem=in_sem.at[p],
                        device_id={"dp": to},
                        device_id_type=MESH,
                    ).start()

    corr_ref[...] = msgs[...]
    kept.wait()
    for copy in hops:
        copy.wait_send()
    for p in range(2):
        for _, copy in copies[p]:
            copy.wait_send()
        many = pl.ds(0, quad * (tall - 1))
        pltpu.make_async_copy(landed.at[p, many], landed.at[p, many], send_sem.at[p]).wait()
        many = pl.ds(0, half - 1 + p)
        pltpu.make_async_copy(msgs.at[many], msgs.at[many], out_sem.at[p]).wait()
    for p in range(2):
        many = pl.ds(0, half - 1 + p)
        pltpu.make_async_copy(returned.at[many], returned.at[many], in_sem.at[p]).wait()
    back_ref[...] = returned[...]


def whole(block, ops, shares, groups):
    tiles, eight, width = block.shape
    deep = 8
    half = groups // 2
    blk = (tiles - 1) * eight // 2
    n = NOPS * (blk // shares)
    cols = half * SUB
    vmem = pl.BlockSpec(memory_space=pltpu.VMEM)
    dma = pltpu.SemaphoreType.DMA
    return pl.pallas_call(
        functools.partial(whole_kernel, shares, groups, deep),
        out_shape=(jax.ShapeDtypeStruct((groups, 1, 128), jnp.float32),) * 2,
        in_specs=[vmem, vmem],
        out_specs=[vmem, vmem],
        scratch_shapes=[
            pltpu.VMEM((deep - 1, tiles, eight, width), jnp.bfloat16),
            pltpu.VMEM((deep, groups // deep, eight, width), jnp.bfloat16),
            pltpu.VMEM((2, half, eight, width), jnp.bfloat16),
            pltpu.VMEM((2, NOPS * blk, width), jnp.bfloat16),
            pltpu.VMEM((3, NOPS * blk, width), jnp.bfloat16),
            pltpu.VMEM((2, shares, 6 * n, cols), jnp.float32),
            pltpu.VMEM((2, shares - 1, 6 * n, cols), jnp.float32),
            pltpu.VMEM((groups, 1, 128), jnp.float32),
            pltpu.VMEM((groups, 1, 128), jnp.float32),
            dma((deep,)),
            dma((deep,)),
            dma((2,)),
            dma((2,)),
            dma((deep,)),
            dma((2, shares - 1)),
            dma((2, shares - 1)),
            dma((2,)),
            dma((2,)),
            dma,
        ],
        compiler_params=pltpu.CompilerParams(
            collective_id=0, has_side_effects=True, vmem_limit_bytes=48 * 1024 * 1024
        ),
    )(block, ops)


def shards(intensities, observed, qweights, ops, pick):
    blk, width = intensities.shape
    groups = lax.axis_size("dp")
    shares = lax.axis_size("refl")
    rows = blk // shares
    own_w = (observed.astype(jnp.float32) * qweights.astype(jnp.float32)).astype(jnp.bfloat16)
    asks = jnp.pad(pick.T.astype(jnp.bfloat16), ((0, 7), (0, width - groups)))
    block = jnp.concatenate([intensities, own_w, asks], 0).reshape(-1, 8, width)
    corr, back = whole(block, ops, shares, groups)
    used = SUB * NOPS * rows
    corr = corr[:, 0, :used].reshape(groups, SUB, NOPS, rows).transpose(2, 3, 0, 1)
    corr = corr.reshape(NOPS, rows, groups * SUB)
    back = back[:, 0, :used].reshape(groups, SUB, NOPS, rows)
    returned = back.transpose(2, 0, 1, 3)[:, None]
    return (corr, returned)


def solution(mesh):
    return jax.shard_map(
        shards,
        mesh=mesh,
        in_specs=(
            P("dp", "refl"),
            P("dp", "refl"),
            P("dp", "refl"),
            P(None, "refl"),
            P(None, "dp"),
        ),
        out_specs=(P(None, ("dp", "refl"), None), P(None, "dp", None, None, "refl")),
        check_vma=False,
    )
```

time: 91.9 us -> 76.4 us (0.83)
  Pallas kernels: 84.5 us -> 71 us
  matrix products: 1.66 us -> 0 us
    pallas_call x1, Pallas kernels: 84.5 us -> 71 us  [whole(): pl.pallas_call(functools.partial(whole_kernel, shares, groups, deep), out...]
    dot_general x1 -> x0, matrix products: 1.66 us -> none  [shards(): jnp.dot(chosen, both, preferred_element_type=jnp.float32)]
where the time goes in v4:
time: 76.4 us; the launch traced here: 76.1 us
  Pallas kernels  71 us (93%)
  local copies, waits for them, and re-layouts  2.66 us (3%)
  other arithmetic  1.76 us (2%)
    pallas_call x1, Pallas kernels, whole(): pl.pallas_call(functools.partial(whole_kernel, shares, groups, deep), out...  71 us

profile of v4, /device:TPU:1, one launch (start us, length us, event | category | flops | bytes accessed | tf_op | source)
XLA Modules:
  0.0 76.1 jit_solution(15606311187683732519)
XLA Ops:
  0.6 0.7 convert_bitcast_fusion
  1.3 0.0 copy-start.1
  1.3 1.1 %multiply_convert_fusion = bf16[32,2048]{1,0:T(8,128)(2,1)S(1)} fusion(bf16[32,2048]{1,0:T(8,128)(2,1)} %param.7, s32[32,2048]{1,0:T(8,128)} %param.6), kind=kLoop, calls=%fused_computation.4 | loop fusion | flops 262144 | bytes 524288 | tf_op jit(solution)/shard_map/convert_element_type | solution.py:339
  2.4 0.0 copy-done.1
  2.4 0.0 copy-start
  2.4 0.7 copy-done
  3.1 71.0 %shard_map.68 = (f32[64,1,128]{2,1,0:T(1,128)S(1)}, f32[64,1,128]{2,1,0:T(1,128)S(1)}) custom-call(bf16[9,8,2048]{2,1,0:T(8,128)(2,1)S(1)} %fusion.2.block_ref, s32[4,2048]{1,0:T(4,128)S(1)} %copy-done), custom_call_target="tpu_custom_call" | custom-call | tf_op jit(solution)/shard_map/pallas_call | solution.py:302
  74.2 0.1 copy.9
  74.3 0.1 copy.11
  74.3 0.6 copy.12
  75.0 0.2 copy.10
  75.2 0.9 %reshape.24 = f32[4,4,256]{2,1,0:T(4,128)} reshape(f32[4,4,64,4]{3,2,1,0:T(8,128)S(1)} %copy.10) | data formatting | bytes 32768 | tf_op jit(solution)/shard_map/reshape | solution.py:345
  (1 shorter events, 0.0 us)
Async XLA Ops:
  1.3 1.1 %copy-start.1 = (bf16[32,2048]{1,0:T(8,128)(2,1)S(1)}, bf16[32,2048]{1,0:T(8,128)(2,1)}, u32[]{:S(2)}) copy-start(bf16[32,2048]{1,0:T(8,128)(2,1)} %param.5) | copy-start | bytes 393220
  2.4 0.8 copy-start

commit v5 on v4

--- a/solution.py
+++ b/solution.py
@@ -52,13 +52,15 @@
             barrier, inc=1, device_id={"refl": lax.rem(me_r + t, shares)}, device_id_type=MESH
         )
 
-    @pl.loop(1, groups)
+    @pl.loop(1, tall)
     def _(t):
-        pl.semaphore_signal(
-            barrier, inc=1, device_id={"dp": lax.rem(me_d + t, groups)}, device_id_type=MESH
-        )
-
-    pl.semaphore_wait(barrier, shares - 1 + groups - 1)
+        to = device(lax.rem(me_p + t, tall), me_z)
+        pl.semaphore_signal(barrier, inc=1, device_id={"dp": to}, device_id_type=MESH)
+
+    for t in (1, deep - 1):
+        to = device(me_p, lax.rem(me_z + t, deep))
+        pl.semaphore_signal(barrier, inc=1, device_id={"dp": to}, device_id_type=MESH)
+    pl.semaphore_wait(barrier, shares - 1 + tall - 1 + 2)
     up = device(me_p, lax.rem(me_z + 1, deep))
     down = device(me_p, lax.rem(me_z + deep - 1, deep))
     far = quad - 1
@@ -78,19 +80,17 @@
         copy.start()
         return copy
 
-    def hop_up(j):
+    parts_of = (pl.ds(0, cut), pl.ds(cut, tiles - cut))
+
+    def hop_up(j, h):
         src = block_ref if j == 1 else ring.at[j - 2]
-        if j <= far:
-            return hop(j - 1, src, ring.at[j - 1], up)
-        part = pl.ds(0, cut)
-        return hop(j - 1, src.at[part], ring.at[last, part], up)
-
-    def hop_down(j):
+        dst = ring.at[j - 1 if j <= far else last]
+        return hop(2 * (j - 1) + h, src.at[parts_of[h]], dst.at[parts_of[h]], up)
+
+    def hop_down(j, h):
         src = block_ref if j == 1 else ring.at[far + j - 2]
-        if j <= far:
-            return hop(quad + j - 1, src, ring.at[far + j - 1], down)
-        part = pl.ds(cut, tiles - cut)
-        return hop(quad + j - 1, src.at[part], ring.at[last, part], down)
+        dst = ring.at[far + j - 1 if j <= far else last]
+        return hop(2 * (quad + j - 1) + h, src.at[parts_of[h]], dst.at[parts_of[h]], down)
 
     row_at = lax.broadcasted_iota(jnp.int32, (tall * 8, 128), 0)
     lane_at = lax.broadcasted_iota(jnp.int32, (tall * 8, 128), 1)
@@ -213,16 +213,26 @@
             )
             copy.start()
             copies[p].append((t, copy))
-    hops = [hop_up(1), hop_down(1)]
+    hops = []
+    flying = {}
+
+    def fly(go, j, h):
+        copy = go(j, h)
+        hops.append(copy)
+        flying[go, j, h] = copy
+
+    for h in range(2):
+        fly(hop_up, 1, h)
+        fly(hop_down, 1, 1 - h)
     serve(0, block_ref)
     operate(0)
     operate(1)
     for j in range(1, quad):
-        above, below = hops[-2:]
-        above.wait_recv()
-        hops.append(hop_up(j + 1))
-        below.wait_recv()
-        hops.append(hop_down(j + 1))
+        for h in range(2):
+            for go, part in ((hop_up, h), (hop_down, 1 - h)):
+                flying[go, j, part].wait_recv()
+                if j < far or h == 0:
+                    fly(go, j + 1, part)
         serve(-j, ring.at[j - 1])
         serve(j, ring.at[far + j - 1])
         if j == 1:
@@ -231,8 +241,8 @@
             operate(3)
             weigh()
     sums(0)
-    for copy in hops[-2:]:
-        copy.wait_recv()
+    flying[hop_up, quad, 0].wait_recv()
+    flying[hop_down, quad, 1].wait_recv()
     serve(quad, ring.at[last])
     sums(1)
     kept = pltpu.make_async_copy(msgs.at[me_d], returned.at[me_d], kept_sem)
@@ -314,8 +324,8 @@
             pltpu.VMEM((2, shares - 1, 6 * n, cols), jnp.float32),
             pltpu.VMEM((groups, 1, 128), jnp.float32),
             pltpu.VMEM((groups, 1, 128), jnp.float32),
-            dma((deep,)),
-            dma((deep,)),
+            dma((2 * deep,)),
+            dma((2 * deep,)),
             dma((2,)),
             dma((2,)),
             dma((deep,)),

time: 76.4 us -> 72 us (0.942)
  Pallas kernels: 71 us -> 66.7 us
    pallas_call x1, Pallas kernels: 71 us -> 66.7 us  [whole(): pl.pallas_call(functools.partial(whole_kernel, shares, groups, deep), out...]
where the time goes in v5:
time: 72 us; the launch traced here: 71.8 us
  Pallas kernels  66.7 us (93%)
  local copies, waits for them, and re-layouts  2.66 us (4%)
  other arithmetic  1.76 us (2%)
    pallas_call x1, Pallas kernels, whole(): pl.pallas_call(functools.partial(whole_kernel, shares, groups, deep), out...  66.7 us

profile of v5, /device:TPU:1, one launch (start us, length us, event | category | flops | bytes accessed | tf_op | source)
XLA Modules:
  0.0 71.8 jit_solution(3929234759711363343)
XLA Ops:
  0.6 0.7 convert_bitcast_fusion
  1.3 0.0 copy-start.1
  1.3 1.1 %multiply_convert_fusion = bf16[32,2048]{1,0:T(8,128)(2,1)S(1)} fusion(bf16[32,2048]{1,0:T(8,128)(2,1)} %param.7, s32[32,2048]{1,0:T(8,128)} %param.6), kind=kLoop, calls=%fused_computation.4 | loop fusion | flops 262144 | bytes 524288 | tf_op jit(solution)/shard_map/convert_element_type | solution.py:349
  2.4 0.0 copy-done.1
  2.4 0.0 copy-start
  2.4 0.7 %copy-done = s32[4,2048]{1,0:T(4,128)S(1)} copy-done((s32[4,2048]{1,0:T(4,128)S(1)}, s32[4,2048]{1,0:T(4,128)}, u32[]{:S(2)}) %copy-start) | copy-done | bytes 32792
  3.1 66.7 %shard_map.68 = (f32[64,1,128]{2,1,0:T(1,128)S(1)}, f32[64,1,128]{2,1,0:T(1,128)S(1)}) custom-call(bf16[9,8,2048]{2,1,0:T(8,128)(2,1)S(1)} %fusion.2.block_ref, s32[4,2048]{1,0:T(4,128)S(1)} %copy-done), custom_call_target="tpu_custom_call" | custom-call | tf_op jit(solution)/shard_map/pallas_call | solution.py:312
  69.9 0.1 copy.9
  69.9 0.1 copy.11
  70.0 0.6 copy.12
  70.6 0.2 copy.10
  70.9 0.9 %reshape.24 = f32[4,4,256]{2,1,0:T(4,128)} reshape(f32[4,4,64,4]{3,2,1,0:T(8,128)S(1)} %copy.10) | data formatting | bytes 32768 | tf_op jit(solution)/shard_map/reshape | solution.py:355
  (1 shorter events, 0.0 us)
Async XLA Ops:
  1.3 1.1 %copy-start.1 = (bf16[32,2048]{1,0:T(8,128)(2,1)S(1)}, bf16[32,2048]{1,0:T(8,128)(2,1)}, u32[]{:S(2)}) copy-start(bf16[32,2048]{1,0:T(8,128)(2,1)} %param.5) | copy-start | bytes 393220
  2.4 0.8 %copy-start = (s32[4,2048]{1,0:T(4,128)S(1)}, s32[4,2048]{1,0:T(4,128)}, u32[]{:S(2)}) copy-start(s32[4,2048]{1,0:T(4,128)} %ops_ref.1) | copy-start | bytes 98308
